TPU v7x, 32 devices: a whole 2x2x4 slice. The times are simulated.
32 devices in a mesh: ctx: 8 (over z, x), chan: 4 (over y, core).
Axes of the slice: x: 2, y: 2, z: 4, core: 2. Of those that a mesh axis runs over, the one named last changes fastest.
Arguments:
- query_in: bfloat16 [4096, 1024], P('chan', 'ctx'), may hold values from -6 to 6
- key_in: bfloat16 [4096, 1024], P('chan', 'ctx'), may hold values from -6 to 6
- value_in: bfloat16 [4096, 1024], P('chan', 'ctx'), may hold values from -6 to 6
- short_kernel: float32 [3, 3, 4096], P(None, None, 'chan'), may hold values from -3.5 to 3.5
- filter_in: float32 [64, 64], replicated, may hold values from -0.75 to 0.75
- filter_out: float32 [64, 4096], P(None, 'chan'), may hold values from -0.75 to 0.75
- filter_decay: float32 [4096], P('chan'), may hold values from 0.5 to 40
- skip_gain: float32 [4096], P('chan'), may hold values from -3 to 3
- grad_out: bfloat16 [4096, 1024], P('chan', 'ctx'), may hold values from -6 to 6
Outputs:
- output: bfloat16 [4096, 1024], P('chan', 'ctx')
- grad_query: bfloat16 [4096, 1024], P('chan', 'ctx')
- grad_key: bfloat16 [4096, 1024], P('chan', 'ctx')
- grad_value: bfloat16 [4096, 1024], P('chan', 'ctx')
- grad_short: float32 [3, 3, 4096], P(None, None, 'chan')
- grad_filter_in: float32 [64, 64], replicated
- grad_filter_out: float32 [64, 4096], P(None, 'chan')
- grad_decay: float32 [4096], P('chan')
- grad_skip: float32 [4096], P('chan')
All inputs are finite; a program needn't handle non-finite values.
Results may differ from a plain program's by a relative error of at most 0.0006.
Values may be sent and summed in bfloat16 or wider, within the bound.
No kernel may reach another device: no remote copies, remote signals or barrier semaphores. Data moves between devices by JAX's collectives and lax.ppermute only.
A program may use at most 128 MiB of HBM per device.

v0:
```python
import math
import jax
import jax.numpy as jnp
from jax import lax
from jax.sharding import PartitionSpec as P

PRECISE = lax.Precision.HIGHEST


def shifted(value, axis, by):
    peers = lax.axis_size(axis)
    pairs = [(i, i + by) for i in range(peers) if 0 <= i + by < peers]
    return lax.ppermute(value, axis, pairs)


def position_features(position, sequence, feature_rows):
    bands = jnp.arange(feature_rows // 2, dtype=jnp.int32)
    factor = 4 * (bands + 1) * (bands + 1)
    phase = position[None, :] * factor[:, None] % sequence
    angles = 2.0 * math.pi / sequence * phase.astype(jnp.float32)
    return jnp.concatenate([jnp.cos(angles), jnp.sin(angles)], axis=0)


def angle_tables(left_index, right_index, modulus):
    phase = left_index[:, None] * right_index[None, :] % modulus
    angles = 2.0 * math.pi / modulus * phase.astype(jnp.float32)
    return (jnp.cos(angles), jnp.sin(angles))


def contract(form, left, right):
    return jnp.einsum(form, left, right, precision=PRECISE)


def times_forward(real_part, imag_part, cosine, sine):
    return (real_part * cosine + imag_part * sine, imag_part * cosine - real_part * sine)


def times_inverse(real_part, imag_part, cosine, sine):
    return (real_part * cosine - imag_part * sine, imag_part * cosine + real_part * sine)


def complex_times(first_real, first_imag, second_real, second_imag):
    return (
        first_real * second_real - first_imag * second_imag,
        first_real * second_imag + first_imag * second_real,
    )


def local_forward(real_part, imag_part):
    length = real_part.shape[-1]
    inner = 64
    outer = length // inner
    leading = real_part.shape[:-1]
    real_part = real_part.reshape(leading + (outer, inner))
    imag_part = imag_part.reshape(leading + (outer, inner))
    outer_index = jnp.arange(outer, dtype=jnp.int32)
    inner_index = jnp.arange(inner, dtype=jnp.int32)
    cos_outer, sin_outer = angle_tables(outer_index, outer_index, outer)
    first_real = contract("cb,...ba->...ca", cos_outer, real_part) + contract(
        "cb,...ba->...ca", sin_outer, imag_part
    )
    first_imag = contract("cb,...ba->...ca", cos_outer, imag_part) - contract(
        "cb,...ba->...ca", sin_outer, real_part
    )
    cos_middle, sin_middle = angle_tables(outer_index, inner_index, length)
    first_real, first_imag = times_forward(first_real, first_imag, cos_middle, sin_middle)
    cos_inner, sin_inner = angle_tables(inner_index, inner_index, inner)
    final_real = contract("...ca,da->...cd", first_real, cos_inner) + contract(
        "...ca,da->...cd", first_imag, sin_inner
    )
    final_imag = contract("...ca,da->...cd", first_imag, cos_inner) - contract(
        "...ca,da->...cd", first_real, sin_inner
    )
    return (final_real, final_imag)


def local_inverse(real_part, imag_part):
    outer = real_part.shape[-2]
    inner = real_part.shape[-1]
    length = outer * inner
    leading = real_part.shape[:-2]
    outer_index = jnp.arange(outer, dtype=jnp.int32)
    inner_index = jnp.arange(inner, dtype=jnp.int32)
    cos_inner, sin_inner = angle_tables(inner_index, inner_index, inner)
    first_real = contract("...cd,ad->...ca", real_part, cos_inner) - contract(
        "...cd,ad->...ca", imag_part, sin_inner
    )
    first_imag = contract("...cd,ad->...ca", imag_part, cos_inner) + contract(
        "...cd,ad->...ca", real_part, sin_inner
    )
    cos_middle, sin_middle = angle_tables(outer_index, inner_index, length)
    first_real, first_imag = times_inverse(first_real, first_imag, cos_middle, sin_middle)
    cos_outer, sin_outer = angle_tables(outer_index, outer_index, outer)
    final_real = contract("bc,...ca->...ba", cos_outer, first_real) - contract(
        "bc,...ca->...ba", sin_outer, first_imag
    )
    final_imag = contract("bc,...ca->...ba", cos_outer, first_imag) + contract(
        "bc,...ca->...ba", sin_outer, first_real
    )
    return (final_real.reshape(leading + (length,)), final_imag.reshape(leading + (length,)))


def held_frequencies(device):
    return 2 * device + jnp.arange(2, dtype=jnp.int32)


def forward_spectrum(signals):
    shards = lax.axis_size("ctx")
    device = lax.axis_index("ctx")
    signal_count, channels, length = signals.shape
    padded = 2 * shards * length
    columns = lax.all_to_all(
        signals.reshape((1, signal_count, channels, length)),
        "ctx",
        split_axis=3,
        concat_axis=0,
        tiled=True,
    )
    shard_index = jnp.arange(shards, dtype=jnp.int32)
    freq_index = jnp.arange(2 * shards, dtype=jnp.int32)
    cos_table, sin_table = angle_tables(freq_index, shard_index, 2 * shards)
    rows_real = contract("qp,pmgb->qmgb", cos_table, columns)
    rows_imag = -contract("qp,pmgb->qmgb", sin_table, columns)
    arrived = lax.all_to_all(
        jnp.stack([rows_real, rows_imag]), "ctx", split_axis=1, concat_axis=4, tiled=True
    )
    spec_real = arrived[0]
    spec_imag = arrived[1]
    freqs = held_frequencies(device)
    cosine, sine = angle_tables(freqs, jnp.arange(length, dtype=jnp.int32), padded)
    spec_real, spec_imag = times_forward(
        spec_real, spec_imag, cosine[:, None, None, :], sine[:, None, None, :]
    )
    return local_forward(spec_real, spec_imag)


def inverse_columns(spec_real, spec_imag):
    shards = lax.axis_size("ctx")
    device = lax.axis_index("ctx")
    real_part, imag_part = local_inverse(spec_real, spec_imag)
    length = real_part.shape[-1]
    padded = 2 * shards * length
    freqs = held_frequencies(device)
    cosine, sine = angle_tables(freqs, jnp.arange(length, dtype=jnp.int32), padded)
    real_part, imag_part = times_inverse(
        real_part, imag_part, cosine[:, None, None, :], sine[:, None, None, :]
    )
    shard_index = jnp.arange(shards, dtype=jnp.int32)
    arrived = lax.all_to_all(
        jnp.stack([real_part, imag_part]), "ctx", split_axis=4, concat_axis=1, tiled=True
    )
    cos_table, sin_table = angle_tables(
        shard_index, jnp.arange(2 * shards, dtype=jnp.int32), 2 * shards
    )
    columns = contract("pq,qmgb->pmgb", cos_table, arrived[0]) - contract(
        "pq,qmgb->pmgb", sin_table, arrived[1]
    )
    return columns * (1.0 / padded)


def to_tokens(columns):
    arrived = lax.all_to_all(columns, "ctx", split_axis=0, concat_axis=3, tiled=True)
    return arrived[0]


def body(
    query_in,
    key_in,
    value_in,
    short_kernel,
    filter_in,
    filter_out,
    filter_decay,
    skip_gain,
    grad_out,
):
    shards = lax.axis_size("ctx")
    device = lax.axis_index("ctx")
    length = query_in.shape[1]
    sequence = shards * length
    scale = sequence ** (-0.5)
    inputs = jnp.stack([query_in, key_in, value_in])
    rim = shifted(inputs[:, :, -2:], "ctx", 1)
    values = inputs.astype(jnp.float32)
    rim_values = rim.astype(jnp.float32)
    before_one = jnp.concatenate([rim_values[..., 1:], values[..., :-1]], axis=-1)
    before_two = jnp.concatenate([rim_values, values[..., :-2]], axis=-1)
    kernel = short_kernel[:, :, :, None]
    shorted = kernel[:, 0] * values + kernel[:, 1] * before_one + kernel[:, 2] * before_two
    query_short = shorted[0]
    key_short = shorted[1]
    value_short = shorted[2]
    gate = key_short * value_short
    position = device * length + jnp.arange(length, dtype=jnp.int32)
    fraction = position.astype(jnp.float32) / sequence
    basis = position_features(position, sequence, filter_in.shape[0])
    preact = jnp.dot(filter_in.T, basis, precision=PRECISE)
    hidden = jnp.sin(preact)
    window = jnp.exp(-filter_decay[:, None] * fraction[None, :])
    taps = window * jnp.dot(filter_out.T, hidden, precision=PRECISE) * scale
    spec_real, spec_imag = forward_spectrum(jnp.stack([gate, taps]))
    gate_real, gate_imag = (spec_real[:, 0], spec_imag[:, 0])
    taps_real, taps_imag = (spec_real[:, 1], spec_imag[:, 1])
    prod_real, prod_imag = complex_times(gate_real, gate_imag, taps_real, taps_imag)
    conv = to_tokens(inverse_columns(prod_real[:, None], prod_imag[:, None]))[0]
    mixed = conv + skip_gain[:, None] * gate
    output = (query_short * mixed).astype(jnp.bfloat16)
    upstream = grad_out.astype(jnp.float32)
    grad_mixed = upstream * query_short
    grad_query_short = upstream * mixed
    upper_real, upper_imag = forward_spectrum(grad_mixed[None])
    upper_real = upper_real[:, 0]
    upper_imag = upper_imag[:, 0]
    along_real, along_imag = complex_times(taps_real, -taps_imag, upper_real, upper_imag)
    cross_real, cross_imag = complex_times(gate_real, -gate_imag, upper_real, upper_imag)
    backward = to_tokens(
        inverse_columns(
            jnp.stack([along_real, cross_real], axis=1), jnp.stack([along_imag, cross_imag], axis=1)
        )
    )
    grad_gate = backward[0] + skip_gain[:, None] * grad_mixed
    grad_taps = backward[1]
    grads = jnp.stack([grad_query_short, grad_gate * value_short, grad_gate * key_short])
    after = shifted(grads[..., :2], "ctx", -1)
    next_one = jnp.concatenate([grads[..., 1:], after[..., :1]], axis=-1)
    next_two = jnp.concatenate([grads[..., 2:], after], axis=-1)
    grad_inputs = (kernel[:, 0] * grads + kernel[:, 1] * next_one + kernel[:, 2] * next_two).astype(
        jnp.bfloat16
    )
    short_terms = jnp.stack(
        [
            jnp.sum(grads * values, axis=-1),
            jnp.sum(grads * before_one, axis=-1),
            jnp.sum(grads * before_two, axis=-1),
        ],
        axis=1,
    )
    weighted = grad_taps * window * scale
    out_terms = jnp.dot(hidden, weighted.T, precision=PRECISE)
    grad_hidden = jnp.dot(filter_out, weighted, precision=PRECISE)
    in_terms = jnp.dot(basis, (grad_hidden * jnp.cos(preact)).T, precision=PRECISE)
    decay_terms = jnp.sum(grad_taps * taps * -fraction[None, :], axis=1)
    skip_terms = jnp.sum(grad_mixed * gate, axis=1)
    short_sum, out_sum, decay_sum, skip_sum = lax.psum(
        (short_terms, out_terms, decay_terms, skip_terms), "ctx"
    )
    in_sum = lax.psum(in_terms, ("ctx", "chan"))
    return (
        output,
        grad_inputs[0],
        grad_inputs[1],
        grad_inputs[2],
        short_sum * scale,
        in_sum * scale,
        out_sum * scale,
        decay_sum * scale,
        skip_sum * scale,
    )


def solution(mesh):
    placed = (
        P("chan", "ctx"),
        P("chan", "ctx"),
        P("chan", "ctx"),
        P(None, None, "chan"),
        P(),
        P(None, "chan"),
        P("chan"),
        P("chan"),
        P("chan", "ctx"),
    )
    return jax.shard_map(
        body,
        mesh=mesh,
        in_specs=placed,
        out_specs=(
            P("chan", "ctx"),
            P("chan", "ctx"),
            P("chan", "ctx"),
            P("chan", "ctx"),
            P(None, None, "chan"),
            P(),
            P(None, "chan"),
            P("chan"),
            P("chan"),
        ),
        check_vma=False,
    )
```

profile of v0, /device:TPU:0, one launch (start us, length us, event | category | flops | bytes accessed | tf_op | source)
XLA Modules:
  0.0 651.2 jit_solution(13803028707653949594)
XLA Ops:
  11.0 4.8 collective-permute-start
  20.5 6.6 %all-to-all-start.4 = ((f32[1,1,1024,128]{2,1,0,3:T(1,128)}), f32[1,1,1024,128]{2,1,0,3:T(1,128)}, u32[]{:S(2)}, u32[]{:S(2)}) async-start(f32[1,1,1024,128]{2,1,0,3:T(1,128)} %copy.246), calls=%async_computation.4 | async-start | bytes 1048576 | tf_op jit(solution)/shard_map/all_to_all | solution.py:112
  32.8 7.8 %all-to-all-done.4 = f32[1,1,1024,128]{2,1,0,3:T(1,128)} async-done(((f32[1,1,1024,128]{2,1,0,3:T(1,128)}), f32[1,1,1024,128]{2,1,0,3:T(1,128)}, u32[]{:S(2)}, u32[]{:S(2)}) %all-to-all-start.4) | async-done | bytes 524320 | tf_op jit(solution)/shard_map/all_to_all | solution.py:112
  40.6 4.2 all-to-all-start
  48.6 2.6 copy.248
  51.2 18.4 %all-to-all-done = f32[1,2,1024,128]{2,1,0,3:T(2,128)} async-done(((f32[1,2,1024,128]{2,1,0,3:T(2,128)}), f32[1,2,1024,128]{2,1,0,3:T(2,128)}, u32[]{:S(2)}, u32[]{:S(2)}) %all-to-all-start) | async-done | bytes 1048608 | tf_op jit(solution)/shard_map/all_to_all | solution.py:112
  69.6 4.8 all-to-all-start.5
  74.4 3.4 negate_bitcast_fusion
  77.9 3.4 convolution_bitcast_fusion
  81.9 4.4 copy.220
  86.3 35.7 %all-to-all-done.5 = f32[2,16,1,1024,16]{3,4,2,0,1:T(8,128)} async-done(((f32[2,16,1,1024,16]{3,4,2,0,1:T(8,128)}), f32[2,16,1,1024,16]{3,4,2,0,1:T(8,128)}, u32[]{:S(2)}, u32[]{:S(2)}) %all-to-all-start.5) | async-done | bytes 2097184 | tf_op jit(solution)/shard_map/all_to_all | solution.py:124
  122.0 4.7 all-to-all-start.1
  132.9 4.1 fusion.61
  136.9 4.3 fusion.35
  141.3 4.1 fusion.65
  145.3 5.7 subtract_bitcast_fusion.1
  152.6 2.5 fusion.34
  155.1 2.4 fusion.55
  157.5 61.7 %all-to-all-done.1 = f32[2,16,2,1024,16]{3,4,2,0,1:T(8,128)} async-done(((f32[2,16,2,1024,16]{3,4,2,0,1:T(8,128)}), f32[2,16,2,1024,16]{3,4,2,0,1:T(8,128)}, u32[]{:S(2)}, u32[]{:S(2)}) %all-to-all-start.1) | async-done | bytes 4194336 | tf_op jit(solution)/shard_map/all_to_all | solution.py:124
  219.3 2.5 copy.221
  224.1 7.9 %fusion.26 = f32[2,2,1024,64,2]{2,4,3,1,0:T(2,128)S(1)} fusion(f32[2,2,1024,2,64]{2,4,3,1,0:T(8,128)S(1)} %get-tuple-element.68), kind=kOutput, calls=%fused_computation.48 | convolution fusion | flops 12582968 | bytes 4194304 | tf_op jit(solution)/shard_map/cb,...ba->...ca/dot_general | solution.py:31
  232.0 8.3 %fusion.22 = f32[2,2,1024,64,2]{2,4,3,1,0:T(2,128)S(1)} fusion(f32[2,2,1024,2,64]{2,4,3,1,0:T(8,128)S(1)} %get-tuple-element.69), kind=kOutput, calls=%fused_computation.44 | convolution fusion | flops 12582968 | bytes 4194304 | tf_op jit(solution)/shard_map/cb,...ba->...ca/dot_general | solution.py:31
  240.3 8.2 %convolution_add_fusion = f32[2,2,1024,64,2]{2,4,3,1,0:T(2,128)S(1)} fusion(f32[2,2,1024,64,2]{2,4,3,1,0:T(2,128)S(1)} %fusion.26, f32[2,2,1024,2,64]{2,4,3,1,0:T(8,128)S(1)} %get-tuple-element.69), kind=kOutput, calls=%fused_computation.42 | convolution fusion | flops 13107256 | bytes 6291456 | tf_op jit(solution)/shard_map/cb,...ba->...ca/dot_general | solution.py:31
  248.6 11.2 %fusion.2 = (f32[2,2,1024,2,64]{2,3,4,1,0:T(2,128)S(1)}, f32[2,2,1024,2,64]{2,3,4,1,0:T(2,128)S(1)}) fusion(f32[2,2,1024,64,2]{2,4,3,1,0:T(2,128)S(1)} %convolution_add_fusion, f32[2,64]{0,1:T(8,128)S(1)} %copy-done.21, f32[2,64]{0,1:T(8,128)S(1)} %copy-done.23, f32[2,2,1024,64,2]{2,4,3,1,0:T(2,128)S(1)} %fusion.22, ...), kind=kOutput, calls=%fused_computation.14 | convolution fusion | flops 16252984 | bytes 10486784 | tf_op jit(solution)/shard_map/cb,...ba->...ca/dot_general | solution.py:31
  259.7 2.8 fusion.4
  262.6 2.8 fusion.6
  265.4 3.1 fusion.16
  268.6 3.1 fusion.19
  271.7 3.9 multiply_subtract_fusion.3
  280.2 2.4 fusion.12
  284.9 9.6 %multiply_subtract_fusion = (f32[2,2,1024,2,64]{2,3,4,1,0:T(2,128)S(1)}, f32[2,2,1024,2,64]{2,3,4,1,0:T(2,128)S(1)}) fusion(f32[2,64]{0,1:T(8,128)S(1)} %copy-done.21, f32[2,64]{0,1:T(8,128)S(1)} %copy-done.23, f32[2,2,1024,2,64]{2,4,3,1,0:T(8,128)S(1)} %fusion.13, f32[2,2,1024,2,64]{2,4,3,1,0:T(8,128)S(1)} %fusion.15, ...), kind=kLoop, calls=%fused_computation.23 | loop fusion | flops 4194304 | bytes 12583936 | tf_op jit(solution)/shard_map/sub | solution.py:39
  294.5 7.5 %fusion.190 = f32[2,2,1024,64,2]{2,4,3,1,0:T(2,128)S(1)} fusion(f32[2,2,1024,2,64]{2,3,4,1,0:T(2,128)S(1)} %get-tuple-element.60), kind=kOutput, calls=%fused_computation.283 | convolution fusion | flops 12582968 | bytes 4194304 | tf_op jit(solution)/shard_map/bc,...ca->...ba/dot_general | solution.py:31
  302.0 7.5 %fusion.188 = f32[2,2,1024,64,2]{2,4,3,1,0:T(2,128)S(1)} fusion(f32[2,2,1024,2,64]{2,3,4,1,0:T(2,128)S(1)} %get-tuple-element.61), kind=kOutput, calls=%fused_computation.281 | convolution fusion | flops 12582968 | bytes 4194304 | tf_op jit(solution)/shard_map/bc,...ca->...ba/dot_general | solution.py:31
  309.6 8.4 %subtract_bitcast_fusion = f32[2,2,1024,2,64]{2,3,4,1,0:T(2,128)S(1)} fusion(f32[2,2,1024,64,2]{2,4,3,1,0:T(2,128)S(1)} %fusion.190, f32[2,2,1024,2,64]{2,3,4,1,0:T(2,128)S(1)} %get-tuple-element.61), kind=kOutput, calls=%fused_computation.21 | convolution fusion | flops 13107256 | bytes 6291456 | tf_op jit(solution)/shard_map/bc,...ca->...ba/dot_general | solution.py:31
  317.9 8.0 %add_bitcast_fusion = f32[2,2,1024,2,64]{2,3,4,1,0:T(2,128)S(1)} fusion(f32[2,2,1024,64,2]{2,4,3,1,0:T(2,128)S(1)} %fusion.188, f32[2,2,1024,2,64]{2,3,4,1,0:T(2,128)S(1)} %get-tuple-element.60), kind=kOutput, calls=%fused_computation.20 | convolution fusion | flops 13107256 | bytes 6291456 | tf_op jit(solution)/shard_map/bc,...ca->...ba/dot_general | solution.py:31
  328.8 5.2 copy.268
  334.0 5.0 all-to-all-start.6
  339.0 2.6 fusion.45
  345.8 4.1 fusion.67
  349.8 4.3 fusion.37
  354.5 4.1 fusion.71
  358.5 4.4 fusion.38
  363.8 2.9 copy.240
  366.8 64.8 %all-to-all-done.6 = f32[2,2,2,1024,128]{3,2,1,0,4:T(2,128)} async-done(((f32[2,2,2,1024,128]{3,2,1,0,4:T(2,128)}), f32[2,2,2,1024,128]{3,2,1,0,4:T(2,128)}, u32[]{:S(2)}, u32[]{:S(2)}) %all-to-all-start.6) | async-done | bytes 4194336 | tf_op jit(solution)/shard_map/all_to_all | solution.py:149
  431.5 4.4 all-to-all-start.2
  435.9 4.6 copy.269
  442.3 3.0 copy.271
  445.3 3.7 squeeze.65
  449.1 4.6 copy.270
  453.7 3.7 squeeze.64
  457.3 2.9 fusion.137
  462.9 20.8 %all-to-all-done.2 = f32[2,2,1,1024,128]{3,1,2,0,4:T(2,128)} async-done(((f32[2,2,1,1024,128]{3,1,2,0,4:T(2,128)}), f32[2,2,1,1024,128]{3,1,2,0,4:T(2,128)}, u32[]{:S(2)}, u32[]{:S(2)}) %all-to-all-start.2) | async-done | bytes 2097184 | tf_op jit(solution)/shard_map/all_to_all | solution.py:149
  483.7 4.5 all-to-all-start.7
  488.2 2.8 copy.241
  493.9 2.9 reshape.382
  496.9 3.0 copy.242
  499.9 2.9 reshape.381
  506.5 7.3 %all-to-all-done.7 = f32[8,2,1024,16]{2,3,1,0:T(8,128)} async-done(((f32[8,2,1024,16]{2,3,1,0:T(8,128)}), f32[8,2,1024,16]{2,3,1,0:T(8,128)}, u32[]{:S(2)}, u32[]{:S(2)}) %all-to-all-start.7) | async-done | bytes 1048608 | tf_op jit(solution)/shard_map/all_to_all | solution.py:162
  513.8 4.1 all-to-all-start.3
  523.4 40.9 %psum.36 = f32[64,64]{1,0:T(8,128)S(1)} all-reduce(f32[64,64]{1,0:T(8,128)} %fusion.105), channel_id=1, replica_groups=mesh['ctx'=8,'chan'=4] {'ctx','chan'}, use_global_device_ids=true, to_apply=%region_4.5 | all-reduce | flops 4096 | bytes 32768 | tf_op jit(solution)/shard_map/psum | solution.py:247
  567.0 2.8 fusion.73
  574.1 37.3 %all-reduce = (f32[3,3,1024]{2,0,1:T(4,128)S(1)}, f32[1024]{0:T(1024)S(1)}, f32[1024]{0:T(1024)S(1)}) all-reduce(f32[3,3,1024]{2,0,1:T(4,128)S(1)} %pad_maximum_fusion.14, f32[1024]{0:T(1024)S(1)} %get-tuple-element.106, f32[1024]{0:T(1024)S(1)} %get-tuple-element.96), channel_id=1, replica_groups=mesh['ctx'=8,'chan'=4] {'ctx'}, use_global_device_ids=true, to_apply=%region_3.4 | all-reduce | flops 11264 | bytes 90112 | tf_op jit(solution)/shard_map/psum | solution.py:244
  615.0 2.7 collective-permute-done.1
  621.0 21.3 %all-reduce.3.cloned.1.call-done = f32[64,1024]{1,0:T(8,128)} async-done(((f32[64,1024]{1,0:T(8,128)}), f32[64,1024]{1,0:T(8,128)}) %all-reduce.3.cloned.1.call-update) | async-done | bytes 262160 | tf_op jit(solution)/shard_map/psum | solution.py:244
  (172 shorter events, 75.1 us)
Async XLA Ops:
  7.2 22.2 %copy-start = (f32[64,1024]{1,0:T(8,128)S(1)}, f32[64,1024]{1,0:T(8,128)}, u32[]{:S(2)}) copy-start(f32[64,1024]{1,0:T(8,128)} %param.14) | copy-start | bytes 786436
  8.3 2.6 copy-start.10
  8.3 7.5 %copy-start.27 = (f32[3,3,1024]{2,1,0:T(4,128)S(1)}, f32[3,3,1024]{2,1,0:T(4,128)}, u32[]{:S(2)}) copy-start(f32[3,3,1024]{2,1,0:T(4,128)} %param.12) | copy-start | bytes 110596
  8.3 7.7 %copy-start.36 = (f32[1024]{0:T(1024)S(1)}, f32[1024]{0:T(1024)}, u32[]{:S(2)}) copy-start(f32[1024]{0:T(1024)} %param.15) | copy-start | bytes 12292
  8.4 7.8 %copy-start.19 = (bf16[1024,128]{1,0:T(8,128)(2,1)S(1)}, bf16[1024,128]{1,0:T(8,128)(2,1)}, u32[]{:S(2)}) copy-start(bf16[1024,128]{1,0:T(8,128)(2,1)} %param.17) | copy-start | bytes 786436
  9.6 7.4 %copy-start.11 = (bf16[1024,128]{0,1:T(8,128)(2,1)}, bf16[1024,128]{0,1:T(8,128)(2,1)S(1)}, u32[]{:S(2)}) copy-start(bf16[1024,128]{0,1:T(8,128)(2,1)S(1)} %copy.215) | copy-start | bytes 786436
  10.8 6.5 copy-start.12
  11.0 6.2 collective-permute-start
  17.3 1.8 copy-start.25
  17.3 1.7 copy-start.18
  20.5 20.0 %all-to-all-start.4 = ((f32[1,1,1024,128]{2,1,0,3:T(1,128)}), f32[1,1,1024,128]{2,1,0,3:T(1,128)}, u32[]{:S(2)}, u32[]{:S(2)}) async-start(f32[1,1,1024,128]{2,1,0,3:T(1,128)} %copy.246), calls=%async_computation.4 | async-start | bytes 1048576 | tf_op jit(solution)/shard_map/all_to_all | solution.py:112
  27.7 1.7 copy-start.37
  30.1 0.8 copy-start.8
  40.6 29.0 %all-to-all-start = ((f32[1,2,1024,128]{2,1,0,3:T(2,128)}), f32[1,2,1024,128]{2,1,0,3:T(2,128)}, u32[]{:S(2)}, u32[]{:S(2)}) async-start(f32[1,2,1024,128]{2,1,0,3:T(2,128)} %copy.217), calls=%async_computation | async-start | bytes 2097152 | tf_op jit(solution)/shard_map/all_to_all | solution.py:112
  69.6 52.4 %all-to-all-start.5 = ((f32[2,16,1,1024,16]{3,4,2,0,1:T(8,128)}), f32[2,16,1,1024,16]{3,4,2,0,1:T(8,128)}, u32[]{:S(2)}, u32[]{:S(2)}) async-start(f32[2,16,1,1024,16]{3,4,2,0,1:T(8,128)} %copy.248), calls=%async_computation.5 | async-start | bytes 4194304 | tf_op jit(solution)/shard_map/all_to_all | solution.py:124
  122.0 97.3 %all-to-all-start.1 = ((f32[2,16,2,1024,16]{3,4,2,0,1:T(8,128)}), f32[2,16,2,1024,16]{3,4,2,0,1:T(8,128)}, u32[]{:S(2)}, u32[]{:S(2)}) async-start(f32[2,16,2,1024,16]{3,4,2,0,1:T(8,128)} %copy.220), calls=%async_computation.1 | async-start | bytes 8388608 | tf_op jit(solution)/shard_map/all_to_all | solution.py:124
  127.4 2.1 copy-start.30
  130.3 2.2 copy-start.28
  141.2 4.1 copy-start.20
  141.2 4.1 copy-start.22
  151.1 4.0 copy-start.15
  222.6 0.7 copy-start.29
  240.3 8.3 %copy-start.21 = (f32[2,64]{0,1:T(8,128)S(1)}, f32[2,64]{0,1:T(8,128)}, u32[]{:S(2)}) copy-start(f32[2,64]{0,1:T(8,128)} %copy.229) | copy-start | bytes 1540
  240.3 8.3 %copy-start.23 = (f32[2,64]{0,1:T(8,128)S(1)}, f32[2,64]{0,1:T(8,128)}, u32[]{:S(2)}) copy-start(f32[2,64]{0,1:T(8,128)} %copy.226) | copy-start | bytes 1540
  268.5 3.1 copy-start.14
  268.6 3.1 copy-start.16
  268.6 3.1 copy-start.17
  326.5 0.7 copy-start.33
  326.5 0.7 copy-start.34
  334.0 97.5 %all-to-all-start.6 = ((f32[2,2,2,1024,128]{3,2,1,0,4:T(2,128)}), f32[2,2,2,1024,128]{3,2,1,0,4:T(2,128)}, u32[]{:S(2)}, u32[]{:S(2)}) async-start(f32[2,2,2,1024,128]{3,2,1,0,4:T(2,128)} %copy.268), calls=%async_computation.6 | async-start | bytes 8388608 | tf_op jit(solution)/shard_map/all_to_all | solution.py:149
  339.0 2.6 copy-start.1
  339.0 3.8 copy-start.2
  342.9 1.3 copy-start.31
  342.9 1.3 copy-start.32
  358.5 4.7 copy-start.35
  431.5 52.2 %all-to-all-start.2 = ((f32[2,2,1,1024,128]{3,1,2,0,4:T(2,128)}), f32[2,2,1,1024,128]{3,1,2,0,4:T(2,128)}, u32[]{:S(2)}, u32[]{:S(2)}) async-start(f32[2,2,1,1024,128]{3,1,2,0,4:T(2,128)} %copy.240), calls=%async_computation.2 | async-start | bytes 4194304 | tf_op jit(solution)/shard_map/all_to_all | solution.py:149
  457.3 2.9 copy-start.3
  483.7 30.1 %all-to-all-start.7 = ((f32[8,2,1024,16]{2,3,1,0:T(8,128)}), f32[8,2,1024,16]{2,3,1,0:T(8,128)}, u32[]{:S(2)}, u32[]{:S(2)}) async-start(f32[8,2,1024,16]{2,3,1,0:T(8,128)} %copy.272), calls=%async_computation.7 | async-start | bytes 2097152 | tf_op jit(solution)/shard_map/all_to_all | solution.py:162
  502.8 2.0 copy-start.13
  513.8 53.3 %all-to-all-start.3 = ((f32[8,1,1024,16]{2,3,1,0:T(8,128)}), f32[8,1,1024,16]{2,3,1,0:T(8,128)}, u32[]{:S(2)}, u32[]{:S(2)}) async-start(f32[8,1,1024,16]{2,3,1,0:T(8,128)} %copy.244), calls=%async_computation.3 | async-start | bytes 1048576 | tf_op jit(solution)/shard_map/all_to_all | solution.py:162
  517.9 124.3 %all-reduce.3.cloned.1.call-start = ((), (), s32[]{:S(2)}) async-start(), calls=%async_computation.8 | async-start | bytes 524288 | tf_op jit(solution)/shard_map/psum | solution.py:244
  518.0 2.2 copy-start.9
  518.0 3.9 copy-start.24
  521.1 0.8 copy-start.7
  567.0 4.7 copy-start.26
  612.0 5.7 collective-permute-start.1
  614.1 3.7 copy-start.4
  614.1 3.7 copy-start.5
  614.1 3.7 copy-start.6
Sparse Core Ops, SparseCore 0:
  571.8 70.4 all-reduce.2
where the time goes:
time: 659 us; the launch traced here: 651 us
  waiting for transfers between devices  241 us (37%)
  matrix products  162 us (25%)
  local copies, waits for them, and re-layouts  82.3 us (12%)
  blocking collectives  78.2 us (12%)
  starting transfers between devices  44.5 us (7%)
  other arithmetic  28.1 us (4%)
  between operations  15.7 us (2%)
    dot_general x40, matrix products, contract(): return jnp.einsum(form, left, right, precision=PRECISE)  156 us
    all_to_all x2, waiting for transfers between devices, forward_spectrum(): lax.all_to_all(jnp.stack([rows_real, rows_imag]), 'ctx', split_axis=1, co...  97.4 us
    all_to_all x2, waiting for transfers between devices, inverse_columns(): lax.all_to_all(jnp.stack([real_part, imag_part]), 'ctx', split_axis=4, co...  85.6 us
    psum x1, blocking collectives, body(): in_sum = lax.psum(in_terms, ('ctx', 'chan'))  40.9 us
    psum x1, blocking collectives, body(): lax.psum((short_terms, out_terms, decay_terms, skip_terms), 'ctx')  37.3 us
    all_to_all x2, waiting for transfers between devices, forward_spectrum(): lax.all_to_all(signals.reshape((1, signal_count, channels, length)), 'ctx...  26.2 us
    psum x1, waiting for transfers between devices, body(): lax.psum((short_terms, out_terms, decay_terms, skip_terms), 'ctx')  21.3 us
  transfers between devices with their start and end apart: 11, of which 10 were waited for; matrix products, arithmetic and copies ran while one was open for 22% of the time, Pallas kernels for 0%

commit v1 on v0

--- a/solution.py
+++ b/solution.py
@@ -1,3 +1,4 @@
+import functools
 import math
 import jax
 import jax.numpy as jnp
@@ -5,6 +6,38 @@
 from jax.sharding import PartitionSpec as P
 
 PRECISE = lax.Precision.HIGHEST
+
+
+def treat_members_all_on(slab_in, join_dim, block_in):
+    reached = slab_in.shape
+    aux = slab_in.reshape(
+        *reached[:join_dim], block_in, reached[join_dim] // block_in, *reached[join_dim + 1 :]
+    )
+    return jnp.moveaxis(aux, join_dim, 0)
+
+
+def _assign_tasks(mat, along_dim):
+    current_arr = list(mat.shape[1:])
+    current_arr[along_dim] *= mat.shape[0]
+    return jnp.moveaxis(mat, 0, along_dim).reshape(current_arr)
+
+
+def choose_the_blocks(work_x, net_axis, field, panel):
+    e_now = jax.lax.axis_size(net_axis)
+    f_now = jax.lax.axis_index(net_axis)
+    all_values, met_up = (e_now, f_now)
+    w_next = treat_members_all_on(work_x, field, all_values)
+    frames = [w_next[met_up]]
+    for d in [*range(1, all_values)]:
+        even = w_next[met_up ^ d]
+        big = jax.lax.ppermute(even, net_axis, [(b, b ^ d) for b in range(all_values)])
+        frames.append(big)
+    m_next = jnp.stack(frames, axis=0)
+    w_next = m_next[met_up ^ jnp.arange(all_values)]
+    return _assign_tasks(w_next, panel)
+
+
+_obtain_map = functools.partial(choose_the_blocks, net_axis="ctx", field=1, panel=4)
 
 
 def shifted(value, axis, by):
@@ -121,9 +154,7 @@
     cos_table, sin_table = angle_tables(freq_index, shard_index, 2 * shards)
     rows_real = contract("qp,pmgb->qmgb", cos_table, columns)
     rows_imag = -contract("qp,pmgb->qmgb", sin_table, columns)
-    arrived = lax.all_to_all(
-        jnp.stack([rows_real, rows_imag]), "ctx", split_axis=1, concat_axis=4, tiled=True
-    )
+    arrived = _obtain_map(jnp.stack([rows_real, rows_imag]))
     spec_real = arrived[0]
     spec_imag = arrived[1]
     freqs = held_frequencies(device)

time: 659 us -> 743 us (1.13)
  starting transfers between devices: 44.5 us -> 93.4 us
  waiting for transfers between devices: 241 us -> 282 us
  matrix products: 162 us -> 153 us
    all_to_all x2 -> x0, waiting for transfers between devices: 97.4 us -> none  [forward_spectrum(): lax.all_to_all(jnp.stack([rows_real, rows_imag]), 'ctx', split_axis=1, co...]
    ppermute x0 -> x14, waiting for transfers between devices: none -> 91.5 us  [choose_the_blocks(): jax.lax.ppermute(even, net_axis, [(b, b ^ d) for b in range(all_values)])]
    psum x1, waiting for transfers between devices: 21.3 us -> 66.1 us  [body(): lax.psum((short_terms, out_terms, decay_terms, skip_terms), 'ctx')]
    ppermute x0 -> x14, starting transfers between devices: none -> 43.8 us  [choose_the_blocks(): jax.lax.ppermute(even, net_axis, [(b, b ^ d) for b in range(all_values)])]
    all_to_all x2, waiting for transfers between devices: 7.28 us -> 28 us  [to_tokens(): lax.all_to_all(columns, 'ctx', split_axis=0, concat_axis=3, tiled=True)]
    all_to_all x2, starting transfers between devices: 9.33 us -> 25.8 us  [inverse_columns(): lax.all_to_all(jnp.stack([real_part, imag_part]), 'ctx', split_axis=4, co...]
    all_to_all x2, waiting for transfers between devices: 26.2 us -> 9.97 us  [forward_spectrum(): lax.all_to_all(signals.reshape((1, signal_count, channels, length)), 'ctx...]
    all_to_all x2 -> x0, starting transfers between devices: 9.55 us -> none  [forward_spectrum(): lax.all_to_all(jnp.stack([rows_real, rows_imag]), 'ctx', split_axis=1, co...]
  transfers between devices with their start and end apart: 11 -> 23, of which waited for: 10 -> 13; matrix products, arithmetic and copies ran while one was open for 22% -> 17% of each run, Pallas kernels for 0% -> 0%
where the time goes in v1:
time: 743 us; the launch traced here: 738 us
  waiting for transfers between devices  282 us (38%)
  matrix products  153 us (21%)
  starting transfers between devices  93.4 us (13%)
  local copies, waits for them, and re-layouts  83.7 us (11%)
  blocking collectives  74.8 us (10%)
  other arithmetic  34.8 us (5%)
  between operations  15.9 us (2%)
    dot_general x40, matrix products, contract(): return jnp.einsum(form, left, right, precision=PRECISE)  149 us
    ppermute x14, waiting for transfers between devices, choose_the_blocks(): jax.lax.ppermute(even, net_axis, [(b, b ^ d) for b in range(all_values)])  91.5 us
    all_to_all x2, waiting for transfers between devices, inverse_columns(): lax.all_to_all(jnp.stack([real_part, imag_part]), 'ctx', split_axis=4, co...  86.8 us
    psum x1, waiting for transfers between devices, body(): lax.psum((short_terms, out_terms, decay_terms, skip_terms), 'ctx')  66.1 us
    ppermute x14, starting transfers between devices, choose_the_blocks(): jax.lax.ppermute(even, net_axis, [(b, b ^ d) for b in range(all_values)])  43.8 us
    psum x1, blocking collectives, body(): in_sum = lax.psum(in_terms, ('ctx', 'chan'))  39.2 us
    psum x1, blocking collectives, body(): lax.psum((short_terms, out_terms, decay_terms, skip_terms), 'ctx')  35.7 us
    all_to_all x2, waiting for transfers between devices, to_tokens(): lax.all_to_all(columns, 'ctx', split_axis=0, concat_axis=3, tiled=True)  28 us
  transfers between devices with their start and end apart: 23, of which 13 were waited for; matrix products, arithmetic and copies ran while one was open for 17% of the time, Pallas kernels for 0%

profile of v1, /device:TPU:0, one launch (start us, length us, event | category | flops | bytes accessed | tf_op | source)
XLA Modules:
  0.0 737.8 jit_solution(18120003627878602156)
XLA Ops:
  11.0 4.8 collective-permute-start
  23.9 4.9 all-to-all-start.3
  33.1 10.0 %all-to-all-done.3 = f32[1,1,1024,128]{2,1,0,3:T(1,128)S(1)} async-done(((f32[1,1,1024,128]{2,1,0,3:T(1,128)}), f32[1,1,1024,128]{2,1,0,3:T(1,128)S(1)}, u32[]{:S(2)}, u32[]{:S(2)}) %all-to-all-start.3) | async-done | bytes 524320 | tf_op jit(solution)/shard_map/all_to_all | solution.py:145
  43.1 4.1 all-to-all-start
  56.8 3.0 collective-permute-start.11
  62.1 3.9 collective-permute-done.8
  65.9 5.2 collective-permute-start.13
  71.2 11.0 %collective-permute-start.14 = (f32[2,2,1,1024,16]{3,4,1,0,2:T(8,128)S(1)}, f32[2,2,1,1024,16]{3,4,1,0,2:T(8,128)S(1)}, u32[]{:S(2)}, u32[]{:S(2)}) collective-permute-start(f32[2,2,1,1024,16]{3,4,1,0,2:T(8,128)S(1)} %bitcast.502), channel_id=1, source_target_pairs={{0,28},{4,24},{8,20},{12,16},{16,12},{20,8},{24,4},{28,0},{1,29},{... | collective-permute-start | bytes 786440 | tf_op jit(solution)/shard_map/ppermute | solution.py:33
  82.2 2.9 collective-permute-done.10
  85.1 17.3 %collective-permute-done.11 = f32[2,2,1,1024,16]{3,4,1,0,2:T(8,128)S(1)} collective-permute-done((f32[2,2,1,1024,16]{3,4,1,0,2:T(8,128)S(1)}, f32[2,2,1,1024,16]{3,4,1,0,2:T(8,128)S(1)}, u32[]{:S(2)}, u32[]{:S(2)}) %collective-permute-start.11) | collective-permute-done | bytes 262176 | tf_op jit(solution)/shard_map/ppermute | solution.py:33
  102.5 6.1 collective-permute-done.12
  110.0 2.4 gather_fusion.1
  113.6 4.1 fusion.60
  117.7 4.2 fusion.34
  121.9 4.2 fusion.64
  126.2 5.4 subtract_bitcast_fusion.1
  133.1 2.5 fusion.54
  142.5 4.4 fusion.73
  148.0 2.5 fusion.33
  150.6 10.4 %collective-permute-start.2 = (f32[2,2,2,1024,16]{3,4,2,1,0:T(8,128)S(1)}, f32[2,2,2,1024,16]{3,4,2,1,0:T(8,128)S(1)}, u32[]{:S(2)}, u32[]{:S(2)}) collective-permute-start(f32[2,2,2,1024,16]{3,4,2,1,0:T(8,128)S(1)} %bitcast.494), channel_id=1, source_target_pairs={{0,8},{4,12},{8,0},{12,4},{16,24},{20,28},{24,16},{28,20},{1,9},{5... | collective-permute-start | bytes 1572872 | tf_op jit(solution)/shard_map/ppermute | solution.py:33
  170.0 22.5 %collective-permute-done.2 = f32[2,2,2,1024,16]{3,4,2,1,0:T(8,128)S(1)} collective-permute-done((f32[2,2,2,1024,16]{3,4,2,1,0:T(8,128)S(1)}, f32[2,2,2,1024,16]{3,4,2,1,0:T(8,128)S(1)}, u32[]{:S(2)}, u32[]{:S(2)}) %collective-permute-start.2) | collective-permute-done | bytes 524320 | tf_op jit(solution)/shard_map/ppermute | solution.py:33
  192.5 2.4 collective-permute-start.7
  195.7 8.1 %collective-permute-done.3 = f32[2,2,2,1024,16]{3,4,2,1,0:T(8,128)S(1)} collective-permute-done((f32[2,2,2,1024,16]{3,4,2,1,0:T(8,128)S(1)}, f32[2,2,2,1024,16]{3,4,2,1,0:T(8,128)S(1)}, u32[]{:S(2)}, u32[]{:S(2)}) %collective-permute-start.3) | collective-permute-done | bytes 524320 | tf_op jit(solution)/shard_map/ppermute | solution.py:33
  205.5 30.8 %collective-permute-done.5 = f32[2,2,2,1024,16]{3,4,2,1,0:T(8,128)S(1)} collective-permute-done((f32[2,2,2,1024,16]{3,4,2,1,0:T(8,128)S(1)}, f32[2,2,2,1024,16]{3,4,2,1,0:T(8,128)S(1)}, u32[]{:S(2)}, u32[]{:S(2)}) %collective-permute-start.5) | collective-permute-done | bytes 524320 | tf_op jit(solution)/shard_map/ppermute | solution.py:33
  238.8 5.1 gather_fusion
  244.0 2.5 fusion.407
  247.8 7.9 %fusion.26 = f32[2,2,1024,64,2]{2,4,3,1,0:T(2,128)S(1)} fusion(f32[2,2,1024,2,64]{2,4,3,1,0:T(8,128)S(1)} %get-tuple-element.77), kind=kOutput, calls=%fused_computation.80 | convolution fusion | flops 12582968 | bytes 4194304 | tf_op jit(solution)/shard_map/cb,...ba->...ca/dot_general | solution.py:64
  255.7 8.0 %fusion.22 = f32[2,2,1024,64,2]{2,4,3,1,0:T(2,128)S(1)} fusion(f32[2,2,1024,2,64]{2,4,3,1,0:T(8,128)S(1)} %get-tuple-element.78), kind=kOutput, calls=%fused_computation.76 | convolution fusion | flops 12582968 | bytes 4194304 | tf_op jit(solution)/shard_map/cb,...ba->...ca/dot_general | solution.py:64
  263.7 8.2 %convolution_add_fusion = f32[2,2,1024,64,2]{2,4,3,1,0:T(2,128)S(1)} fusion(f32[2,2,1024,64,2]{2,4,3,1,0:T(2,128)S(1)} %fusion.26, f32[2,2,1024,2,64]{2,4,3,1,0:T(8,128)S(1)} %get-tuple-element.78), kind=kOutput, calls=%fused_computation.73 | convolution fusion | flops 13107256 | bytes 6291456 | tf_op jit(solution)/shard_map/cb,...ba->...ca/dot_general | solution.py:64
  272.0 10.8 %fusion.2 = (f32[2,2,1024,2,64]{2,3,4,1,0:T(2,128)S(1)}, f32[2,2,1024,2,64]{2,3,4,1,0:T(2,128)S(1)}) fusion(f32[2,2,1024,64,2]{2,4,3,1,0:T(2,128)S(1)} %convolution_add_fusion, f32[2,64]{0,1:T(8,128)S(1)} %copy-done.35, f32[2,64]{0,1:T(8,128)S(1)} %copy.290, f32[2,2,1024,64,2]{2,4,3,1,0:T(2,128)S(1)} %fusion.22, ...), kind=kOutput, calls=%fused_computation.46 | convolution fusion | flops 16252984 | bytes 10486784 | tf_op jit(solution)/shard_map/cb,...ba->...ca/dot_general | solution.py:64
  282.8 2.8 fusion.6
  285.7 2.8 fusion.4
  288.5 3.1 fusion.16
  291.7 3.1 fusion.19
  294.8 2.7 multiply_subtract_fusion.3
  306.8 9.4 %multiply_subtract_fusion = (f32[2,2,1024,2,64]{2,3,4,1,0:T(2,128)S(1)}, f32[2,2,1024,2,64]{2,3,4,1,0:T(2,128)S(1)}) fusion(f32[2,64]{0,1:T(8,128)S(1)} %copy-done.35, f32[2,64]{0,1:T(8,128)S(1)} %copy.290, f32[2,2,1024,2,64]{2,4,3,1,0:T(8,128)S(1)} %fusion.13, f32[2,2,1024,2,64]{2,4,3,1,0:T(8,128)S(1)} %fusion.15, f32[2,2,1024,2,64]{2,4,3,1,0:T(8,128)S(1)} %fusion.14, ...), kind=kLoop, calls=%fused_computation.55 | loop fusion | flops 4194304 | bytes 12583936 | tf_op jit(solution)/shard_map/sub | solution.py:72
  316.2 7.5 %fusion.248 = f32[2,2,1024,64,2]{2,4,3,1,0:T(2,128)S(1)} fusion(f32[2,2,1024,2,64]{2,3,4,1,0:T(2,128)S(1)} %get-tuple-element.69), kind=kOutput, calls=%fused_computation.407 | convolution fusion | flops 12582968 | bytes 4194304 | tf_op jit(solution)/shard_map/bc,...ca->...ba/dot_general | solution.py:64
  323.8 7.5 %fusion.246 = f32[2,2,1024,64,2]{2,4,3,1,0:T(2,128)S(1)} fusion(f32[2,2,1024,2,64]{2,3,4,1,0:T(2,128)S(1)} %get-tuple-element.70), kind=kOutput, calls=%fused_computation.405 | convolution fusion | flops 12582968 | bytes 4194304 | tf_op jit(solution)/shard_map/bc,...ca->...ba/dot_general | solution.py:64
  331.3 8.4 %subtract_bitcast_fusion = f32[2,2,1024,2,64]{2,3,4,1,0:T(2,128)S(1)} fusion(f32[2,2,1024,64,2]{2,4,3,1,0:T(2,128)S(1)} %fusion.248, f32[2,2,1024,2,64]{2,3,4,1,0:T(2,128)S(1)} %get-tuple-element.70), kind=kOutput, calls=%fused_computation.53 | convolution fusion | flops 13107256 | bytes 6291456 | tf_op jit(solution)/shard_map/bc,...ca->...ba/dot_general | solution.py:64
  340.3 8.0 %add_bitcast_fusion = f32[2,2,1024,2,64]{2,3,4,1,0:T(2,128)S(1)} fusion(f32[2,2,1024,64,2]{2,4,3,1,0:T(2,128)S(1)} %fusion.246, f32[2,2,1024,2,64]{2,3,4,1,0:T(2,128)S(1)} %get-tuple-element.69), kind=kOutput, calls=%fused_computation.52 | convolution fusion | flops 13107256 | bytes 6291456 | tf_op jit(solution)/shard_map/bc,...ca->...ba/dot_general | solution.py:64
  350.5 5.3 copy.332
  355.8 22.2 %all-to-all-start.4 = ((f32[2,2,2,1024,128]{3,2,1,0,4:T(2,128)}), f32[2,2,2,1024,128]{3,2,1,0,4:T(2,128)}, u32[]{:S(2)}, u32[]{:S(2)}) async-start(f32[2,2,2,1024,128]{3,2,1,0,4:T(2,128)} %copy.332), calls=%async_computation.4 | async-start | bytes 8388608 | tf_op jit(solution)/shard_map/all_to_all | solution.py:180
  383.3 4.1 fusion.70
  387.4 4.3 fusion.37
  392.0 4.1 fusion.66
  396.1 4.7 fusion.36
  401.7 2.9 copy.304
  404.6 65.3 %all-to-all-done.4 = f32[2,2,2,1024,128]{3,2,1,0,4:T(2,128)} async-done(((f32[2,2,2,1024,128]{3,2,1,0,4:T(2,128)}), f32[2,2,2,1024,128]{3,2,1,0,4:T(2,128)}, u32[]{:S(2)}, u32[]{:S(2)}) %all-to-all-start.4) | async-done | bytes 4194336 | tf_op jit(solution)/shard_map/all_to_all | solution.py:180
  469.9 3.6 all-to-all-start.1
  473.6 4.6 copy.333
  480.0 2.9 copy.334
  483.0 3.7 squeeze.120
  486.6 4.5 copy.335
  491.1 3.7 squeeze.121
  494.8 2.9 fusion.191
  500.5 21.6 %all-to-all-done.1 = f32[2,2,1,1024,128]{3,1,2,0,4:T(2,128)S(1)} async-done(((f32[2,2,1,1024,128]{3,1,2,0,4:T(2,128)}), f32[2,2,1,1024,128]{3,1,2,0,4:T(2,128)S(1)}, u32[]{:S(2)}, u32[]{:S(2)}) %all-to-all-start.1) | async-done | bytes 2097184 | tf_op jit(solution)/shard_map/all_to_all | solution.py:180
  522.0 4.4 all-to-all-start.5
  535.5 16.5 %all-to-all-done.5 = f32[8,2,1024,16]{2,3,1,0:T(8,128)} async-done(((f32[8,2,1024,16]{2,3,1,0:T(8,128)}), f32[8,2,1024,16]{2,3,1,0:T(8,128)}, u32[]{:S(2)}, u32[]{:S(2)}) %all-to-all-start.5) | async-done | bytes 1048608 | tf_op jit(solution)/shard_map/all_to_all | solution.py:193
  552.1 4.1 all-to-all-start.2
  558.8 11.5 %all-to-all-done.2 = f32[8,1,1024,16]{2,3,1,0:T(8,128)} async-done(((f32[8,1,1024,16]{2,3,1,0:T(8,128)}), f32[8,1,1024,16]{2,3,1,0:T(8,128)}, u32[]{:S(2)}, u32[]{:S(2)}) %all-to-all-start.2) | async-done | bytes 524320 | tf_op jit(solution)/shard_map/all_to_all | solution.py:193
  573.9 35.7 %all-reduce = (f32[3,3,1024]{2,0,1:T(4,128)S(1)}, f32[1024]{0:T(1024)S(1)}, f32[1024]{0:T(1024)S(1)}) all-reduce(f32[3,3,1024]{2,0,1:T(4,128)S(1)} %pad_maximum_fusion.12, f32[1024]{0:T(1024)S(1)} %get-tuple-element.131, f32[1024]{0:T(1024)S(1)} %get-tuple-element.121), channel_id=1, replica_groups=mesh['ctx'=8,'chan'=4] {'ctx'}, use_global_device_ids=true, to_apply=%region_3.4 | all-reduce | flops 11264 | bytes 90112 | tf_op jit(solution)/shard_map/psum | solution.py:275
  613.5 39.2 %psum.36 = f32[64,64]{1,0:T(8,128)S(1)} all-reduce(f32[64,64]{1,0:T(8,128)S(1)} %fusion.120), channel_id=1, replica_groups=mesh['ctx'=8,'chan'=4] {'ctx','chan'}, use_global_device_ids=true, to_apply=%region_4.5 | all-reduce | flops 4096 | bytes 32768 | tf_op jit(solution)/shard_map/psum | solution.py:278
  658.1 2.4 fusion.30
  663.1 66.1 %all-reduce.3.cloned.1.call-done = f32[64,1024]{1,0:T(8,128)} async-done(((f32[64,1024]{1,0:T(8,128)}), f32[64,1024]{1,0:T(8,128)}) %all-reduce.3.cloned.1.call-update) | async-done | bytes 262160 | tf_op jit(solution)/shard_map/psum | solution.py:275
  (267 shorter events, 106.8 us)
Async XLA Ops:
  7.2 22.6 %copy-start = (f32[64,1024]{1,0:T(8,128)S(1)}, f32[64,1024]{1,0:T(8,128)}, u32[]{:S(2)}) copy-start(f32[64,1024]{1,0:T(8,128)} %param.14) | copy-start | bytes 786436
  8.3 2.6 copy-start.12
  8.3 7.6 %copy-start.40 = (f32[3,3,1024]{2,1,0:T(4,128)S(1)}, f32[3,3,1024]{2,1,0:T(4,128)}, u32[]{:S(2)}) copy-start(f32[3,3,1024]{2,1,0:T(4,128)} %param.12) | copy-start | bytes 110596
  9.5 11.0 %copy-start.14 = (bf16[1024,128]{0,1:T(8,128)(2,1)}, bf16[1024,128]{0,1:T(8,128)(2,1)S(1)}, u32[]{:S(2)}) copy-start(bf16[1024,128]{0,1:T(8,128)(2,1)S(1)} %copy.279) | copy-start | bytes 786436
  9.6 9.3 %copy-start.49 = (f32[1024]{0:T(1024)S(1)}, f32[1024]{0:T(1024)}, u32[]{:S(2)}) copy-start(f32[1024]{0:T(1024)} %param.15) | copy-start | bytes 12292
  9.6 10.1 %copy-start.24 = (bf16[1024,128]{1,0:T(8,128)(2,1)S(1)}, bf16[1024,128]{1,0:T(8,128)(2,1)}, u32[]{:S(2)}) copy-start(bf16[1024,128]{1,0:T(8,128)(2,1)} %param.17) | copy-start | bytes 786436
  10.8 9.8 %copy-start.16 = (bf16[1024,128]{0,1:T(8,128)(2,1)}, bf16[1024,128]{0,1:T(8,128)(2,1)S(1)}, u32[]{:S(2)}) copy-start(bf16[1024,128]{0,1:T(8,128)(2,1)S(1)} %copy.280) | copy-start | bytes 786436
  11.0 11.4 %copy-start.2 = (f32[3,1024,128]{1,2,0:T(8,128)}, f32[3,1024,128]{1,2,0:T(8,128)S(1)}, u32[]{:S(2)}) copy-start(f32[3,1024,128]{1,2,0:T(8,128)S(1)} %get-tuple-element.129) | copy-start | bytes 4718596
  11.0 9.5 %collective-permute-start = (bf16[3,1024,2]{1,2,0:T(2,128)(2,1)S(1)}, bf16[3,1024,2]{1,2,0:T(2,128)(2,1)S(1)}, u32[]{:S(2)}, u32[]{:S(2)}) collective-permute-start(bf16[3,1024,2]{1,2,0:T(2,128)(2,1)S(1)} %slice.143), channel_id=1, source_target_pairs={{0,4},{4,8},{8,12},{12,16},{16,20},{20,24},{24,28},{1,5},{5,9},{9,... | collective-permute-start | bytes 36872 | tf_op jit(solution)/shard_map/ppermute | solution.py:46
  15.9 4.7 copy-start.42
  15.9 4.7 copy-start.44
  18.1 4.4 copy-start.25
  18.1 4.4 copy-start.27
  18.2 10.6 %copy-start.31 = (f32[32,128]{1,0:T(8,128)}, f32[32,128]{1,0:T(8,128)S(1)}, u32[]{:S(2)}) copy-start(f32[32,128]{1,0:T(8,128)S(1)} %get-tuple-element.137) | copy-start | bytes 49156
  18.2 10.6 %copy-start.33 = (f32[32,128]{1,0:T(8,128)}, f32[32,128]{1,0:T(8,128)S(1)}, u32[]{:S(2)}) copy-start(f32[32,128]{1,0:T(8,128)S(1)} %get-tuple-element.138) | copy-start | bytes 49156
  18.9 3.6 copy-start.29
  22.5 8.0 %copy-start.4 = (f32[3,1024,128]{1,2,0:T(8,128)}, f32[3,1024,128]{1,2,0:T(8,128)S(1)}, u32[]{:S(2)}) copy-start(f32[3,1024,128]{1,2,0:T(8,128)S(1)} %multiply_add_fusion.2) | copy-start | bytes 4718596
  22.6 6.3 copy-start.39
  22.6 7.2 copy-start.52
  23.9 19.1 %all-to-all-start.3 = ((f32[1,1,1024,128]{2,1,0,3:T(1,128)}), f32[1,1,1024,128]{2,1,0,3:T(1,128)S(1)}, u32[]{:S(2)}, u32[]{:S(2)}) async-start(f32[1,1,1024,128]{2,1,0,3:T(1,128)} %copy.310), calls=%async_computation.3 | async-start | bytes 1048576 | tf_op jit(solution)/shard_map/all_to_all | solution.py:145
  28.8 19.7 %copy-start.50 = (s32[8,2]{0,1:T(2,128)}, s32[8,2]{0,1:T(2,128)S(1)}, u32[]{:S(2)}) copy-start(s32[8,2]{0,1:T(2,128)S(1)} %multiply_add_fusion.9) | copy-start | bytes 196
  43.1 92.5 %all-to-all-start = ((f32[1,2,1024,128]{2,1,0,3:T(2,128)}), f32[1,2,1024,128]{2,1,0,3:T(2,128)S(1)}, u32[]{:S(2)}, u32[]{:S(2)}) async-start(f32[1,2,1024,128]{2,1,0,3:T(2,128)} %copy.281), calls=%async_computation | async-start | bytes 2097152 | tf_op jit(solution)/shard_map/all_to_all | solution.py:145
  52.9 13.0 %collective-permute-start.8 = (f32[2,2,1,1024,16]{3,4,1,0,2:T(8,128)S(1)}, f32[2,2,1,1024,16]{3,4,1,0,2:T(8,128)S(1)}, u32[]{:S(2)}, u32[]{:S(2)}) collective-permute-start(f32[2,2,1,1024,16]{3,4,1,0,2:T(8,128)S(1)} %bitcast.506), channel_id=1, source_target_pairs={{0,4},{4,0},{8,12},{12,8},{16,20},{20,16},{24,28},{28,24},{1,5},{5... | collective-permute-start | bytes 786440 | tf_op jit(solution)/shard_map/ppermute | solution.py:33
  55.1 16.1 %collective-permute-start.9 = (f32[2,2,1,1024,16]{3,4,1,0,2:T(8,128)S(1)}, f32[2,2,1,1024,16]{3,4,1,0,2:T(8,128)S(1)}, u32[]{:S(2)}, u32[]{:S(2)}) collective-permute-start(f32[2,2,1,1024,16]{3,4,1,0,2:T(8,128)S(1)} %bitcast.503), channel_id=1, source_target_pairs={{0,8},{4,12},{8,0},{12,4},{16,24},{20,28},{24,16},{28,20},{1,9},{5... | collective-permute-start | bytes 786440 | tf_op jit(solution)/shard_map/ppermute | solution.py:33
  56.7 28.4 %collective-permute-start.10 = (f32[2,2,1,1024,16]{3,4,1,0,2:T(8,128)S(1)}, f32[2,2,1,1024,16]{3,4,1,0,2:T(8,128)S(1)}, u32[]{:S(2)}, u32[]{:S(2)}) collective-permute-start(f32[2,2,1,1024,16]{3,4,1,0,2:T(8,128)S(1)} %bitcast.501), channel_id=1, source_target_pairs={{0,12},{4,8},{8,4},{12,0},{16,28},{20,24},{24,20},{28,16},{1,13},{... | collective-permute-start | bytes 786440 | tf_op jit(solution)/shard_map/ppermute | solution.py:33
  56.8 45.7 %collective-permute-start.11 = (f32[2,2,1,1024,16]{3,4,1,0,2:T(8,128)S(1)}, f32[2,2,1,1024,16]{3,4,1,0,2:T(8,128)S(1)}, u32[]{:S(2)}, u32[]{:S(2)}) collective-permute-start(f32[2,2,1,1024,16]{3,4,1,0,2:T(8,128)S(1)} %bitcast.500), channel_id=1, source_target_pairs={{0,16},{4,20},{8,24},{12,28},{16,0},{20,4},{24,8},{28,12},{1,17},{... | collective-permute-start | bytes 786440 | tf_op jit(solution)/shard_map/ppermute | solution.py:33
  60.4 48.1 %collective-permute-start.12 = (f32[2,2,1,1024,16]{3,4,1,0,2:T(8,128)S(1)}, f32[2,2,1,1024,16]{3,4,1,0,2:T(8,128)S(1)}, u32[]{:S(2)}, u32[]{:S(2)}) collective-permute-start(f32[2,2,1,1024,16]{3,4,1,0,2:T(8,128)S(1)} %bitcast.504), channel_id=1, source_target_pairs={{0,20},{4,16},{8,28},{12,24},{16,4},{20,0},{24,12},{28,8},{1,21},{... | collective-permute-start | bytes 786440 | tf_op jit(solution)/shard_map/ppermute | solution.py:33
  65.9 42.7 %collective-permute-start.13 = (f32[2,2,1,1024,16]{3,4,1,0,2:T(8,128)S(1)}, f32[2,2,1,1024,16]{3,4,1,0,2:T(8,128)S(1)}, u32[]{:S(2)}, u32[]{:S(2)}) collective-permute-start(f32[2,2,1,1024,16]{3,4,1,0,2:T(8,128)S(1)} %bitcast.505), channel_id=1, source_target_pairs={{0,24},{4,28},{8,16},{12,20},{16,8},{20,12},{24,0},{28,4},{1,25},{... | collective-permute-start | bytes 786440 | tf_op jit(solution)/shard_map/ppermute | solution.py:33
  71.2 37.4 %collective-permute-start.14 = (f32[2,2,1,1024,16]{3,4,1,0,2:T(8,128)S(1)}, f32[2,2,1,1024,16]{3,4,1,0,2:T(8,128)S(1)}, u32[]{:S(2)}, u32[]{:S(2)}) collective-permute-start(f32[2,2,1,1024,16]{3,4,1,0,2:T(8,128)S(1)} %bitcast.502), channel_id=1, source_target_pairs={{0,28},{4,24},{8,20},{12,16},{16,12},{20,8},{24,4},{28,0},{1,29},{... | collective-permute-start | bytes 786440 | tf_op jit(solution)/shard_map/ppermute | solution.py:33
  121.9 4.3 copy-start.35
  131.6 3.9 copy-start.51
  147.0 20.6 %collective-permute-start.1 = (f32[2,2,2,1024,16]{3,4,2,1,0:T(8,128)S(1)}, f32[2,2,2,1024,16]{3,4,2,1,0:T(8,128)S(1)}, u32[]{:S(2)}, u32[]{:S(2)}) collective-permute-start(f32[2,2,2,1024,16]{3,4,2,1,0:T(8,128)S(1)} %bitcast.495), channel_id=1, source_target_pairs={{0,4},{4,0},{8,12},{12,8},{16,20},{20,16},{24,28},{28,24},{1,5},{5... | collective-permute-start | bytes 1572872 | tf_op jit(solution)/shard_map/ppermute | solution.py:33
  150.6 41.8 %collective-permute-start.2 = (f32[2,2,2,1024,16]{3,4,2,1,0:T(8,128)S(1)}, f32[2,2,2,1024,16]{3,4,2,1,0:T(8,128)S(1)}, u32[]{:S(2)}, u32[]{:S(2)}) collective-permute-start(f32[2,2,2,1024,16]{3,4,2,1,0:T(8,128)S(1)} %bitcast.494), channel_id=1, source_target_pairs={{0,8},{4,12},{8,0},{12,4},{16,24},{20,28},{24,16},{28,20},{1,9},{5... | collective-permute-start | bytes 1572872 | tf_op jit(solution)/shard_map/ppermute | solution.py:33
  162.3 41.5 %collective-permute-start.3 = (f32[2,2,2,1024,16]{3,4,2,1,0:T(8,128)S(1)}, f32[2,2,2,1024,16]{3,4,2,1,0:T(8,128)S(1)}, u32[]{:S(2)}, u32[]{:S(2)}) collective-permute-start(f32[2,2,2,1024,16]{3,4,2,1,0:T(8,128)S(1)} %bitcast.496), channel_id=1, source_target_pairs={{0,12},{4,8},{8,4},{12,0},{16,28},{20,24},{24,20},{28,16},{1,13},{... | collective-permute-start | bytes 1572872 | tf_op jit(solution)/shard_map/ppermute | solution.py:33
  164.2 40.4 %collective-permute-start.4 = (f32[2,2,2,1024,16]{3,4,2,1,0:T(8,128)S(1)}, f32[2,2,2,1024,16]{3,4,2,1,0:T(8,128)S(1)}, u32[]{:S(2)}, u32[]{:S(2)}) collective-permute-start(f32[2,2,2,1024,16]{3,4,2,1,0:T(8,128)S(1)} %bitcast.499), channel_id=1, source_target_pairs={{0,16},{4,20},{8,24},{12,28},{16,0},{20,4},{24,8},{28,12},{1,17},{... | collective-permute-start | bytes 1572872 | tf_op jit(solution)/shard_map/ppermute | solution.py:33
  166.4 69.9 %collective-permute-start.5 = (f32[2,2,2,1024,16]{3,4,2,1,0:T(8,128)S(1)}, f32[2,2,2,1024,16]{3,4,2,1,0:T(8,128)S(1)}, u32[]{:S(2)}, u32[]{:S(2)}) collective-permute-start(f32[2,2,2,1024,16]{3,4,2,1,0:T(8,128)S(1)} %bitcast.497), channel_id=1, source_target_pairs={{0,20},{4,16},{8,28},{12,24},{16,4},{20,0},{24,12},{28,8},{1,21},{... | collective-permute-start | bytes 1572872 | tf_op jit(solution)/shard_map/ppermute | solution.py:33
  167.6 69.5 %collective-permute-start.6 = (f32[2,2,2,1024,16]{3,4,2,1,0:T(8,128)S(1)}, f32[2,2,2,1024,16]{3,4,2,1,0:T(8,128)S(1)}, u32[]{:S(2)}, u32[]{:S(2)}) collective-permute-start(f32[2,2,2,1024,16]{3,4,2,1,0:T(8,128)S(1)} %bitcast.498), channel_id=1, source_target_pairs={{0,24},{4,28},{8,16},{12,20},{16,8},{20,12},{24,0},{28,4},{1,25},{... | collective-permute-start | bytes 1572872 | tf_op jit(solution)/shard_map/ppermute | solution.py:33
  192.5 45.5 %collective-permute-start.7 = (f32[2,2,2,1024,16]{3,4,2,1,0:T(8,128)S(1)}, f32[2,2,2,1024,16]{3,4,2,1,0:T(8,128)S(1)}, u32[]{:S(2)}, u32[]{:S(2)}) collective-permute-start(f32[2,2,2,1024,16]{3,4,2,1,0:T(8,128)S(1)} %bitcast.493), channel_id=1, source_target_pairs={{0,28},{4,24},{8,20},{12,16},{16,12},{20,8},{24,4},{28,0},{1,29},{... | collective-permute-start | bytes 1572872 | tf_op jit(solution)/shard_map/ppermute | solution.py:33
  291.6 3.1 copy-start.18
  291.6 3.1 copy-start.20
  291.6 3.1 copy-start.21
  355.8 114.1 %all-to-all-start.4 = ((f32[2,2,2,1024,128]{3,2,1,0,4:T(2,128)}), f32[2,2,2,1024,128]{3,2,1,0,4:T(2,128)}, u32[]{:S(2)}, u32[]{:S(2)}) async-start(f32[2,2,2,1024,128]{3,2,1,0,4:T(2,128)} %copy.332), calls=%async_computation.4 | async-start | bytes 8388608 | tf_op jit(solution)/shard_map/all_to_all | solution.py:180
  469.9 52.1 %all-to-all-start.1 = ((f32[2,2,1,1024,128]{3,1,2,0,4:T(2,128)}), f32[2,2,1,1024,128]{3,1,2,0,4:T(2,128)S(1)}, u32[]{:S(2)}, u32[]{:S(2)}) async-start(f32[2,2,1,1024,128]{3,1,2,0,4:T(2,128)} %copy.304), calls=%async_computation.1 | async-start | bytes 4194304 | tf_op jit(solution)/shard_map/all_to_all | solution.py:180
  494.8 2.9 copy-start.6
  522.0 30.0 %all-to-all-start.5 = ((f32[8,2,1024,16]{2,3,1,0:T(8,128)}), f32[8,2,1024,16]{2,3,1,0:T(8,128)}, u32[]{:S(2)}, u32[]{:S(2)}) async-start(f32[8,2,1024,16]{2,3,1,0:T(8,128)} %copy.336), calls=%async_computation.5 | async-start | bytes 2097152 | tf_op jit(solution)/shard_map/all_to_all | solution.py:193
  534.4 24.1 %copy-start.11 = (f32[1024,128]{0,1:T(8,128)S(1)}, f32[1024,128]{0,1:T(8,128)}, u32[]{:S(2)}) copy-start(f32[1024,128]{0,1:T(8,128)} %copy-done.10) | copy-start | bytes 1572868
  534.4 24.1 %copy-start.53 = (f32[128]{0:T(128)S(1)}, f32[128]{0:T(128)}, u32[]{:S(2)}) copy-start(f32[128]{0:T(128)} %get-tuple-element.147) | copy-start | bytes 1540
  534.4 24.1 %copy-start.54 = (f32[128]{0:T(128)S(1)}, f32[128]{0:T(128)}, u32[]{:S(2)}) copy-start(f32[128]{0:T(128)} %get-tuple-element.148) | copy-start | bytes 1540
  552.1 18.2 %all-to-all-start.2 = ((f32[8,1,1024,16]{2,3,1,0:T(8,128)}), f32[8,1,1024,16]{2,3,1,0:T(8,128)}, u32[]{:S(2)}, u32[]{:S(2)}) async-start(f32[8,1,1024,16]{2,3,1,0:T(8,128)} %copy.308), calls=%async_computation.2 | async-start | bytes 1048576 | tf_op jit(solution)/shard_map/all_to_all | solution.py:193
  556.2 14.1 %copy-start.5 = (f32[3,1024,128]{1,2,0:T(8,128)S(1)}, f32[3,1024,128]{1,2,0:T(8,128)}, u32[]{:S(2)}) copy-start(f32[3,1024,128]{1,2,0:T(8,128)} %copy-done.4) | copy-start | bytes 4718596
  556.2 14.1 %copy-start.23 = (bf16[1024,128]{0,1:T(8,128)(2,1)S(1)}, bf16[1024,128]{0,1:T(8,128)(2,1)}, u32[]{:S(2)}) copy-start(bf16[1024,128]{0,1:T(8,128)(2,1)} %copy.309) | copy-start | bytes 786436
  556.2 14.1 %copy-start.48 = (f32[1024]{0:T(1024)S(1)}, f32[1024]{0:T(1024)}, u32[]{:S(2)}) copy-start(f32[1024]{0:T(1024)} %param.16) | copy-start | bytes 12292
  556.2 172.9 %all-reduce.3.cloned.1.call-start = ((), (), s32[]{:S(2)}) async-start(), calls=%async_computation.6 | async-start | bytes 524288 | tf_op jit(solution)/shard_map/psum | solution.py:275
  570.3 2.5 copy-start.3
  570.3 2.4 copy-start.13
  570.3 2.4 copy-start.15
  570.3 2.4 copy-start.17
  572.8 39.9 %copy-start.36 = (f32[128,64]{0,1:T(8,128)S(1)}, f32[128,64]{0,1:T(8,128)}, u32[]{:S(2)}) copy-start(f32[128,64]{0,1:T(8,128)} %get-tuple-element.142) | copy-start | bytes 98308
  572.8 40.5 %copy-start.32 = (f32[32,128]{1,0:T(8,128)S(1)}, f32[32,128]{1,0:T(8,128)}, u32[]{:S(2)}) copy-start(f32[32,128]{1,0:T(8,128)} %copy-done.31) | copy-start | bytes 49156
  572.8 40.5 %copy-start.34 = (f32[32,128]{1,0:T(8,128)S(1)}, f32[32,128]{1,0:T(8,128)}, u32[]{:S(2)}) copy-start(f32[32,128]{1,0:T(8,128)} %copy-done.33) | copy-start | bytes 49156
  610.2 47.8 %collective-permute-start.15 = (f32[3,1024,2]{1,2,0:T(2,128)S(1)}, f32[3,1024,2]{1,2,0:T(2,128)S(1)}, u32[]{:S(2)}, u32[]{:S(2)}) collective-permute-start(f32[3,1024,2]{1,2,0:T(2,128)S(1)} %slice.165), channel_id=1, source_target_pairs={{4,0},{8,4},{12,8},{16,12},{20,16},{24,20},{28,24},{5,1},{9,5},{13... | collective-permute-start | bytes 73736 | tf_op jit(solution)/shard_map/ppermute | solution.py:46
  654.2 3.8 copy-start.26
  654.2 3.8 copy-start.28
  654.2 3.8 copy-start.30
  (14 other events, 17.3 us)
Sparse Core Ops, SparseCore 0:
  658.1 70.9 all-reduce.2
